TPU v7x, 32 devices: a whole 2x2x4 slice. The times are simulated.
32 devices in a mesh: ctx: 8 (over z, y), tp: 4 (over x, core).
Axes of the slice: x: 2, y: 2, z: 4, core: 2. Of those that a mesh axis runs over, the one named last changes fastest.
Arguments:
- layer_inputs: bfloat16 [1536, 2048], P('ctx', 'tp'), may hold values from -6 to 6
- states: float32 [1536, 2048], P('ctx', 'tp'), may hold values from -0.7 to 0.7
- cotangent: float32 [1536, 2048], P('ctx', 'tp'), may hold values from -0.009765625 to 0.009765625
- block_weights: float32 [32, 64, 64], P('tp'), may hold values from -1 to 1
Outputs:
- grad_proj: float32 [2048, 2048], P(('ctx', 'tp'))
All inputs are finite; a program needn't handle non-finite values.
Results may differ from a plain program's by a relative error of at most 0.0029.
Values may be sent and summed in bfloat16 or wider, within the bound.
A program may use at most 64 MiB of HBM per device.

v0:
```python
import jax
import jax.numpy as jnp
from jax import lax
from jax.sharding import PartitionSpec as P

exact = lax.Precision.HIGHEST


def from_behind(value, axis, by):
    size = lax.axis_size(axis)
    pairs = [(i, i + by) for i in range(size) if 0 <= i + by < size]
    return lax.ppermute(value, axis, pairs)


def compose(right_map, left_map):
    right_mat, right_vec = right_map
    left_mat, left_vec = left_map
    joined = jnp.einsum("hisj,hjsk->hisk", left_mat, right_mat, precision=exact)
    shifted = left_vec + jnp.einsum("hisj,hjs->his", left_mat, right_vec, precision=exact)
    return (joined, shifted)


def on_device(layer_inputs, states, cotangent, block_weights):
    tokens_here = states.shape[0]
    head_local = block_weights.shape[0]
    head_width = block_weights.shape[1]
    block_len = 32
    blocks = tokens_here // block_len

    def arrange(values):
        shaped = values.reshape(blocks, block_len, head_local, head_width)
        return jnp.transpose(shaped, (1, 2, 3, 0))

    slopes = arrange(1.0 - states * states)
    upstream = arrange(cotangent)

    def build_step(affine_maps, pieces):
        matrices, offsets = affine_maps
        slope_now, grad_now = pieces
        pulled = jnp.einsum("hji,hjsk->hisk", block_weights, matrices, precision=exact)
        matrices = slope_now[..., None] * pulled
        offsets = slope_now * (
            grad_now + jnp.einsum("hji,hjs->his", block_weights, offsets, precision=exact)
        )
        return ((matrices, offsets), None)

    identity_mats = jnp.broadcast_to(
        jnp.eye(head_width, dtype=jnp.float32)[None, :, None, :],
        (head_local, head_width, blocks, head_width),
    )
    zero_offsets = jnp.zeros((head_local, head_width, blocks), jnp.float32)
    (matrices, offsets), unused = lax.scan(
        build_step, (identity_mats, zero_offsets), (slopes, upstream), reverse=True
    )
    flipped = (jnp.flip(matrices, 2), jnp.flip(offsets, 2))
    suffix = lax.associative_scan(compose, flipped, axis=2)
    suffix_mat = jnp.flip(suffix[0], 2)
    suffix_vec = jnp.flip(suffix[1], 2)
    device_mat = suffix_mat[:, :, :1, :]
    device_vec = suffix_vec[:, :, :1]

    def relay_turn(step_index, entering):
        leaving = device_vec + jnp.einsum("hisj,hjs->his", device_mat, entering, precision=exact)
        return from_behind(leaving, "ctx", -1)

    entering = lax.fori_loop(0, lax.axis_size("ctx") - 1, relay_turn, jnp.zeros_like(device_vec))
    later_mat = suffix_mat[:, :, 1:, :]
    later_vector = suffix_vec[:, :, 1:]
    inner_starts = later_vector + jnp.einsum(
        "hisj,hj->his", later_mat, entering[:, :, 0], precision=exact
    )
    starts = jnp.concatenate([inner_starts, entering], axis=2)

    def solve_step(subsequent_step, pieces):
        slope_now, grad_now = pieces
        current = slope_now * (
            grad_now + jnp.einsum("hji,hjs->his", block_weights, subsequent_step, precision=exact)
        )
        return (current, current)

    remaining_part, adjoints = lax.scan(solve_step, starts, (slopes, upstream), reverse=True)
    adjoint_bf = (
        jnp.transpose(adjoints, (1, 2, 3, 0))
        .reshape(head_local * head_width, tokens_here)
        .astype(jnp.bfloat16)
    )
    gathered = lax.all_gather(layer_inputs, "tp", axis=1, tiled=True)
    summed = lax.psum_scatter(
        lax.dot_general(
            gathered, adjoint_bf, (((0,), (1,)), ((), ())), preferred_element_type=jnp.float32
        ),
        "ctx",
        scatter_dimension=0,
        tiled=True,
    )
    result = lax.all_to_all(summed, "tp", split_axis=0, concat_axis=1, tiled=True)
    return result


def solution(mesh):
    in_specs = (P("ctx", "tp"), P("ctx", "tp"), P("ctx", "tp"), P("tp", None, None))
    out_specs = P(("ctx", "tp"), None)
    return jax.shard_map(
        on_device, mesh=mesh, in_specs=in_specs, out_specs=out_specs, check_vma=False
    )
```

profile of v0, /device:TPU:0, one launch (start us, length us, event | category | flops | bytes accessed | tf_op | source)
XLA Modules:
  0.0 375.9 jit_solution(12649809995185188845)
XLA Ops:
  11.1 115.7 %while.45 = (s32[]{:T(128)}, f32[8,64,6,64]{3,1,2,0:T(8,128)S(1)}, f32[8,64,6]{1,2,0:T(8,128)S(1)}, f32[32,8,64,6]{2,3,1,0:T(8,128)}, f32[8,64,64]{2,1,0:T(8,128...) while((s32[]{:T(128)}, f32[8,64,6,64]{3,1,2,0:T(8,128)S(1)}, ...), condition=%wide.region_1.2_spmd.clone, body=%wide.region_0.1_spmd.clone.sunk | while | flops 153560064 | bytes 3518595 | solution.py:52
  12.0 1.5 convolution_multiply_fusion.2
  15.7 1.5 convolution_multiply_fusion.2
  19.3 1.5 convolution_multiply_fusion.2
  22.9 1.5 convolution_multiply_fusion.2
  26.5 1.5 convolution_multiply_fusion.2
  30.1 1.5 convolution_multiply_fusion.2
  37.3 1.5 convolution_multiply_fusion.2
  41.0 1.5 convolution_multiply_fusion.2
  44.6 1.5 convolution_multiply_fusion.2
  48.2 1.5 convolution_multiply_fusion.2
  51.8 1.5 convolution_multiply_fusion.2
  55.4 1.5 convolution_multiply_fusion.2
  59.0 1.5 convolution_multiply_fusion.2
  62.7 1.5 convolution_multiply_fusion.2
  66.3 1.5 convolution_multiply_fusion.2
  69.9 1.5 convolution_multiply_fusion.2
  73.5 1.5 convolution_multiply_fusion.2
  77.1 1.5 convolution_multiply_fusion.2
  80.7 1.5 convolution_multiply_fusion.2
  84.4 1.5 convolution_multiply_fusion.2
  88.0 1.5 convolution_multiply_fusion.2
  91.6 1.5 convolution_multiply_fusion.2
  95.2 1.5 convolution_multiply_fusion.2
  98.8 1.5 convolution_multiply_fusion.2
  102.4 1.5 convolution_multiply_fusion.2
  109.7 1.5 convolution_multiply_fusion.2
  113.3 1.5 convolution_multiply_fusion.2
  124.1 1.5 convolution_multiply_fusion.2
  132.9 8.5 %pad.66 = f32[8,64,5,64]{1,3,2,0:T(8,128)} pad(f32[8,64,3,64]{1,3,2,0:T(8,128)S(1)} %pad_add_fusion, f32[]{:T(128)} %constant.84.clone.1), padding=0_0_0x0_0_0x0_0_1x0_0_0 | pad | bytes 1048580
  141.4 8.6 %pad.33 = f32[8,64,6,64]{1,3,2,0:T(8,128)} pad(f32[8,64,3,64]{1,3,2,0:T(8,128)S(1)} %pad_add_fusion, f32[]{:T(128)} %constant.84.clone.1), padding=0_0_0x0_0_0x1_0_1x0_0_0 | pad | bytes 1179652 | tf_op jit(solution)/shard_map/pad | solution.py:56
  150.0 1.8 convolution_bitcast_fusion.2
  151.7 1.6 copy.30
  155.7 8.5 %pad.32 = f32[8,64,6,64]{1,3,2,0:T(8,128)} pad(f32[8,64,3,64]{1,3,2,0:T(8,128)S(1)} %pad_maximum_fusion, f32[]{:T(128)} %constant.84.clone.1), padding=0_0_0x0_0_0x0_1_1x0_0_0 | pad | bytes 1179652 | tf_op jit(solution)/shard_map/pad | solution.py:56
  165.9 48.5 %while.43 = (s32[]{:T(128)}, f32[8,64,1]{1,0,2:T(8,128)S(1)}, f32[8,64,1]{1,2,0:T(1,128)S(1)}, f32[8,64,1,64]{3,2,1,0:T(1,128)S(1)}, s32[]{:T(128)}) while((s32[]{:T(128)}, f32[8,64,1]{1,0,2:T(8,128)S(1)}, f32[8,64,1]{1,2,0:T(1,128)S(1)}, f32[8,64,1,64]{3,2,1,0:T(1,128)S(1)}, s32[]{:T(128)}) %tuple.93), condition=%wide.region_3.4_spmd, body=%wide.region_2.3_spmd.sunk | while | flops 393730 | bytes 149605 | solution.py:66
  167.8 5.2 %collective-permute-done = f32[8,64,1]{1,0,2:T(8,128)S(1)} collective-permute-done((f32[8,64,1]{1,0,2:T(8,128)S(1)}, f32[8,64,1]{1,0,2:T(8,128)S(1)}, u32[]{:S(2)}, u32[]{:S(2)}) %collective-permute-start) | collective-permute-done | bytes 2080 | tf_op jit(solution)/shard_map/while/body/eval_jaxpr/ppermute | solution.py:12
  174.8 5.1 %collective-permute-done = f32[8,64,1]{1,0,2:T(8,128)S(1)} collective-permute-done((f32[8,64,1]{1,0,2:T(8,128)S(1)}, f32[8,64,1]{1,0,2:T(8,128)S(1)}, u32[]{:S(2)}, u32[]{:S(2)}) %collective-permute-start) | collective-permute-done | bytes 2080 | tf_op jit(solution)/shard_map/while/body/eval_jaxpr/ppermute | solution.py:12
  181.7 5.1 %collective-permute-done = f32[8,64,1]{1,0,2:T(8,128)S(1)} collective-permute-done((f32[8,64,1]{1,0,2:T(8,128)S(1)}, f32[8,64,1]{1,0,2:T(8,128)S(1)}, u32[]{:S(2)}, u32[]{:S(2)}) %collective-permute-start) | collective-permute-done | bytes 2080 | tf_op jit(solution)/shard_map/while/body/eval_jaxpr/ppermute | solution.py:12
  188.6 5.1 %collective-permute-done = f32[8,64,1]{1,0,2:T(8,128)S(1)} collective-permute-done((f32[8,64,1]{1,0,2:T(8,128)S(1)}, f32[8,64,1]{1,0,2:T(8,128)S(1)}, u32[]{:S(2)}, u32[]{:S(2)}) %collective-permute-start) | collective-permute-done | bytes 2080 | tf_op jit(solution)/shard_map/while/body/eval_jaxpr/ppermute | solution.py:12
  195.5 5.1 %collective-permute-done = f32[8,64,1]{1,0,2:T(8,128)S(1)} collective-permute-done((f32[8,64,1]{1,0,2:T(8,128)S(1)}, f32[8,64,1]{1,0,2:T(8,128)S(1)}, u32[]{:S(2)}, u32[]{:S(2)}) %collective-permute-start) | collective-permute-done | bytes 2080 | tf_op jit(solution)/shard_map/while/body/eval_jaxpr/ppermute | solution.py:12
  202.4 5.1 %collective-permute-done = f32[8,64,1]{1,0,2:T(8,128)S(1)} collective-permute-done((f32[8,64,1]{1,0,2:T(8,128)S(1)}, f32[8,64,1]{1,0,2:T(8,128)S(1)}, u32[]{:S(2)}, u32[]{:S(2)}) %collective-permute-start) | collective-permute-done | bytes 2080 | tf_op jit(solution)/shard_map/while/body/eval_jaxpr/ppermute | solution.py:12
  209.4 5.1 %collective-permute-done = f32[8,64,1]{1,0,2:T(8,128)S(1)} collective-permute-done((f32[8,64,1]{1,0,2:T(8,128)S(1)}, f32[8,64,1]{1,0,2:T(8,128)S(1)}, u32[]{:S(2)}, u32[]{:S(2)}) %collective-permute-start) | collective-permute-done | bytes 2080 | tf_op jit(solution)/shard_map/while/body/eval_jaxpr/ppermute | solution.py:12
  214.5 2.2 fusion.24
  217.5 37.3 %while.44 = (s32[]{:T(128)}, f32[8,64,6]{1,2,0:T(8,128)S(1)}, bf16[32,8,64,6]{2,3,1,0:T(8,128)(2,1)S(1)}, f32[32,8,64,6]{2,3,1,0:T(8,128)}, f32[32,8,64,6]{2,3,1...) while((s32[]{:T(128)}, f32[8,64,6]{1,2,0:T(8,128)S(1)}, ...), condition=%wide.region_5.6_spmd, body=%wide.region_4.5_spmd.sunk | while | flops 2365443 | bytes 409709 | solution.py:81
  255.1 8.6 %all_gather.3 = bf16[192,2048]{1,0:T(8,128)(2,1)S(1)} all-gather(bf16[192,512]{1,0:T(8,128)(2,1)S(1)} %copy-done.4), channel_id=1, replica_groups=mesh['ctx'=8,'tp'=4] {'tp'}, dimensions={1}, use_global_device_ids=true | all-gather | bytes 983040 | tf_op jit(solution)/shard_map/all_gather | solution.py:87
  263.7 2.7 convolution_bitcast_fusion
  266.5 89.2 %reduce-scatter.2.cloned.1.call-done = f32[256,512]{0,1:T(8,128)} async-done(((f32[2048,512]{0,1:T(8,128)}), f32[256,512]{0,1:T(8,128)}) %reduce-scatter.2.cloned.1.call-update) | async-done | bytes 524304 | tf_op jit(solution)/shard_map/reduce_scatter | solution.py:88
  356.9 11.4 %all_to_all.19 = f32[4,64,512]{2,1,0:T(8,128)S(1)} all-to-all(f32[4,64,512]{2,1,0:T(8,128)S(1)} %bitcast.157), channel_id=1, replica_groups=mesh['ctx'=8,'tp'=4] {'tp'}, dimensions={0} | all-to-all | bytes 1048576 | tf_op jit(solution)/shard_map/all_to_all | solution.py:96
  (288 shorter events, 138.8 us)
Async XLA Ops:
  6.5 349.1 %reduce-scatter.2.cloned.1.call-start = ((), (), s32[]{:S(2)}) async-start(), calls=%async_computation.2 | async-start | bytes 4718592 | tf_op jit(solution)/shard_map/reduce_scatter | solution.py:88
  7.6 1.7 copy-start.3
  9.4 1.6 copy-start
  130.6 1.1 copy-start.2
  151.7 1.6 slice-start.1
  153.4 1.3 slice-start
  155.7 8.5 %copy-start.1 = (f32[8,64,6,64]{1,3,2,0:T(8,128)S(1)}, f32[8,64,6,64]{1,3,2,0:T(8,128)}, u32[]{:S(2)}) copy-start(f32[8,64,6,64]{1,3,2,0:T(8,128)} %pad.33) | copy-start | bytes 2359300
  166.5 6.5 %collective-permute-start = (f32[8,64,1]{1,0,2:T(8,128)S(1)}, f32[8,64,1]{1,0,2:T(8,128)S(1)}, u32[]{:S(2)}, u32[]{:S(2)}) collective-permute-start(f32[8,64,1]{1,0,2:T(8,128)S(1)} %add_bitcast_fusion.2), channel_id=1, source_target_pairs={{4,0},{8,4},{12,8},{16,12},{20,16},{24,20},{28,24},{5,1},{9,5},{13... | collective-permute-start | bytes 6152 | tf_op jit(solution)/shard_map/while/body/eval_jaxpr/ppermute | solution.py:12
  173.4 6.4 %collective-permute-start = (f32[8,64,1]{1,0,2:T(8,128)S(1)}, f32[8,64,1]{1,0,2:T(8,128)S(1)}, u32[]{:S(2)}, u32[]{:S(2)}) collective-permute-start(f32[8,64,1]{1,0,2:T(8,128)S(1)} %add_bitcast_fusion.2), channel_id=1, source_target_pairs={{4,0},{8,4},{12,8},{16,12},{20,16},{24,20},{28,24},{5,1},{9,5},{13... | collective-permute-start | bytes 6152 | tf_op jit(solution)/shard_map/while/body/eval_jaxpr/ppermute | solution.py:12
  180.4 6.4 %collective-permute-start = (f32[8,64,1]{1,0,2:T(8,128)S(1)}, f32[8,64,1]{1,0,2:T(8,128)S(1)}, u32[]{:S(2)}, u32[]{:S(2)}) collective-permute-start(f32[8,64,1]{1,0,2:T(8,128)S(1)} %add_bitcast_fusion.2), channel_id=1, source_target_pairs={{4,0},{8,4},{12,8},{16,12},{20,16},{24,20},{28,24},{5,1},{9,5},{13... | collective-permute-start | bytes 6152 | tf_op jit(solution)/shard_map/while/body/eval_jaxpr/ppermute | solution.py:12
  187.3 6.4 %collective-permute-start = (f32[8,64,1]{1,0,2:T(8,128)S(1)}, f32[8,64,1]{1,0,2:T(8,128)S(1)}, u32[]{:S(2)}, u32[]{:S(2)}) collective-permute-start(f32[8,64,1]{1,0,2:T(8,128)S(1)} %add_bitcast_fusion.2), channel_id=1, source_target_pairs={{4,0},{8,4},{12,8},{16,12},{20,16},{24,20},{28,24},{5,1},{9,5},{13... | collective-permute-start | bytes 6152 | tf_op jit(solution)/shard_map/while/body/eval_jaxpr/ppermute | solution.py:12
  194.2 6.4 %collective-permute-start = (f32[8,64,1]{1,0,2:T(8,128)S(1)}, f32[8,64,1]{1,0,2:T(8,128)S(1)}, u32[]{:S(2)}, u32[]{:S(2)}) collective-permute-start(f32[8,64,1]{1,0,2:T(8,128)S(1)} %add_bitcast_fusion.2), channel_id=1, source_target_pairs={{4,0},{8,4},{12,8},{16,12},{20,16},{24,20},{28,24},{5,1},{9,5},{13... | collective-permute-start | bytes 6152 | tf_op jit(solution)/shard_map/while/body/eval_jaxpr/ppermute | solution.py:12
  201.1 6.4 %collective-permute-start = (f32[8,64,1]{1,0,2:T(8,128)S(1)}, f32[8,64,1]{1,0,2:T(8,128)S(1)}, u32[]{:S(2)}, u32[]{:S(2)}) collective-permute-start(f32[8,64,1]{1,0,2:T(8,128)S(1)} %add_bitcast_fusion.2), channel_id=1, source_target_pairs={{4,0},{8,4},{12,8},{16,12},{20,16},{24,20},{28,24},{5,1},{9,5},{13... | collective-permute-start | bytes 6152 | tf_op jit(solution)/shard_map/while/body/eval_jaxpr/ppermute | solution.py:12
  208.1 6.4 %collective-permute-start = (f32[8,64,1]{1,0,2:T(8,128)S(1)}, f32[8,64,1]{1,0,2:T(8,128)S(1)}, u32[]{:S(2)}, u32[]{:S(2)}) collective-permute-start(f32[8,64,1]{1,0,2:T(8,128)S(1)} %add_bitcast_fusion.2), channel_id=1, source_target_pairs={{4,0},{8,4},{12,8},{16,12},{20,16},{24,20},{28,24},{5,1},{9,5},{13... | collective-permute-start | bytes 6152 | tf_op jit(solution)/shard_map/while/body/eval_jaxpr/ppermute | solution.py:12
  217.5 37.6 %copy-start.4 = (bf16[192,512]{1,0:T(8,128)(2,1)S(1)}, bf16[192,512]{1,0:T(8,128)(2,1)}, u32[]{:S(2)}) copy-start(bf16[192,512]{1,0:T(8,128)(2,1)} %param.10) | copy-start | bytes 589828
Sparse Core Ops, SparseCore 0:
  266.6 88.9 reduce-scatter.1
where the time goes:
time: 383 us; the launch traced here: 376 us
  matrix products  136 us (36%)
  waiting for transfers between devices  125 us (33%)
  local copies, waits for them, and re-layouts  65 us (17%)
  blocking collectives  20 us (5%)
  between operations  13.7 us (4%)
  starting transfers between devices  9.06 us (2%)
  other arithmetic  4.9 us (1%)
    reduce_scatter x1, waiting for transfers between devices, on_device(): lax.psum_scatter(lax.dot_general(gathered, adjoint_bf, (((0,), (1,)), (()...  89.2 us
    dot_general x32, matrix products, build_step(): jnp.einsum('hji,hjsk->hisk', block_weights, matrices, precision=exact)  48.4 us
    dot_general x32, matrix products, solve_step(): jnp.einsum('hji,hjs->his', block_weights, subsequent_step, precision=exact)  36.3 us
    dot_general x32, matrix products, build_step(): jnp.einsum('hji,hjs->his', block_weights, offsets, precision=exact)  36.1 us
    ppermute x7, waiting for transfers between devices, from_behind(): return lax.ppermute(value, axis, pairs)  35.7 us
    mul x32, local copies, waits for them, and re-layouts, build_step(): matrices = slope_now[..., None] * pulled  24.5 us
    pad x6, local copies, waits for them, and re-layouts, on_device(): suffix = lax.associative_scan(compose, flipped, axis=2)  17.5 us
    unnamed x14, local copies, waits for them, and re-layouts  11.5 us
  transfers between devices with their start and end apart: 8, of which 8 were waited for; matrix products, arithmetic and copies ran while one was open for 0% of the time, Pallas kernels for 0%

commit v1 on v0

v1 whole, which is shorter than its diff:
```python
import functools
import jax
import jax.numpy as jnp
from jax import lax
from jax.experimental import pallas as pl
from jax.experimental.pallas import tpu as pltpu
from jax.sharding import PartitionSpec as P

MESH = pl.DeviceIdType.MESH
CHUNKS = 8
F32 = jnp.float32
BF16 = jnp.bfloat16


def halves(value):
    high = value.astype(BF16)
    low = (value - high.astype(F32)).astype(BF16)
    return high, low


def dot(left, right):
    return jnp.dot(left, right, preferred_element_type=F32)


def dot3(left, right_high, right_low):
    high, low = halves(left)
    return dot(high, right_high) + (dot(low, right_high) + dot(high, right_low))


def block_mask(width, head):
    rows = lax.broadcasted_iota(jnp.int32, (width, width), 0) // head
    cols = lax.broadcasted_iota(jnp.int32, (width, width), 1) // head
    return rows == cols


def recurrence(states_ref, cot_ref, weights_ref, adj_ref,
               maps, offsets, suffix, suffix_vec, spread_e, full, e_in, e_out,
               send_sem, recv_sem):
    n = lax.axis_size("ctx")
    me = lax.axis_index("ctx")
    tokens, units = states_ref.shape
    head = weights_ref.shape[0]
    length = tokens // CHUNKS
    width = min(256, units)
    groups = units // width
    tile = width // head

    barrier = pltpu.get_barrier_semaphore()
    pl.semaphore_signal(barrier, inc=1, device_id={"ctx": lax.rem(me + 1, n)}, device_id_type=MESH)
    pl.semaphore_signal(barrier, inc=1, device_id={"ctx": lax.rem(me + n - 1, n)}, device_id_type=MESH)

    mask = block_mask(width, head)

    def spread(rows):
        return halves(jnp.where(mask, jnp.concatenate([rows] * tile, axis=0), 0.0))

    last = length - 1
    weights = [spread(weights_ref[:, g * width:(g + 1) * width]) for g in range(groups)]

    def token_rows(ref, t):
        return jnp.concatenate([ref[k, pl.ds(t, 1), :] for k in range(CHUNKS)], axis=0)

    def slopes_at(t):
        h = token_rows(states_ref_view, t)
        return 1.0 - h * h

    states_ref_view = states_ref.reshape(CHUNKS, length, units)
    cot_ref_view = cot_ref.reshape(CHUNKS, length, units)
    full_view = full.reshape(CHUNKS, length, units)

    s_last = slopes_at(last)
    offsets[last] = s_last * token_rows(cot_ref_view, last)
    for k in range(CHUNKS):
        maps[last, k * head:(k + 1) * head, :] = weights_ref[...] * s_last[k:k + 1, :]

    def step(i, carry):
        t = last - 1 - i
        s = slopes_at(t)
        c = token_rows(cot_ref_view, t)
        for g in range(groups):
            lanes = slice(g * width, (g + 1) * width)
            high, low = weights[g]
            v = offsets[t + 1, :, lanes]
            offsets[t, :, lanes] = s[:, lanes] * (c[:, lanes] + dot3(v, high, low))
            for k in range(CHUNKS):
                rows = slice(k * head, (k + 1) * head)
                y = dot3(maps[t + 1, rows, lanes], high, low)
                maps[t, rows, lanes] = y * s[k:k + 1, lanes]
        return carry

    lax.fori_loop(0, last, step, 0)

    for g in range(groups):
        lanes = slice(g * width, (g + 1) * width)
        top = (CHUNKS - 1) * head
        running = maps[0, top:top + head, lanes]
        vec = offsets[0, CHUNKS - 1:CHUNKS, lanes]
        suffix[top:top + head, lanes] = running
        suffix_vec[CHUNKS - 1:CHUNKS, lanes] = vec
        for k in range(CHUNKS - 2, -1, -1):
            rows = slice(k * head, (k + 1) * head)
            high, low = spread(maps[0, rows, lanes])
            running = dot3(running, high, low)
            vec = dot3(jnp.broadcast_to(vec, (8, width)), high, low)[0:1] + offsets[0, k:k + 1, lanes]
            suffix[rows, lanes] = running
            suffix_vec[k:k + 1, lanes] = vec

    ones = mask.astype(F32).astype(BF16)
    pick = (lax.broadcasted_iota(jnp.int32, (head, width), 1) % head
            == lax.broadcasted_iota(jnp.int32, (head, width), 0))

    def replicate(row):
        high, low = halves(jnp.where(pick, jnp.broadcast_to(row, (head, width)), 0.0))
        return dot(high, ones) + dot(low, ones)

    pl.semaphore_wait(barrier, 2)
    copy = pltpu.make_async_remote_copy(
        src_ref=e_out, dst_ref=e_in, send_sem=send_sem, recv_sem=recv_sem,
        device_id={"ctx": lax.max(me - 1, 0)}, device_id_type=MESH)

    @pl.when(me == n - 1)
    def _():
        e_in[...] = jnp.zeros_like(e_in)

    @pl.when(me < n - 1)
    def _():
        copy.wait_recv()

    spreads = []
    for g in range(groups):
        lanes = slice(g * width, (g + 1) * width)
        e = replicate(e_in[:, lanes])
        spreads.append(e)
        e_out[:, lanes] = suffix_vec[0:1, lanes] + jnp.sum(
            e * suffix[0:head, lanes], axis=0, keepdims=True)

    @pl.when(me > 0)
    def _():
        copy.start()

    for g in range(groups):
        lanes = slice(g * width, (g + 1) * width)
        e = spreads[g]
        top = (CHUNKS - 1) * head
        spread_e[top:top + head, lanes] = e
        for k in range(1, CHUNKS):
            start = suffix_vec[k:k + 1, lanes] + jnp.sum(
                e * suffix[k * head:(k + 1) * head, lanes], axis=0, keepdims=True)
            spread_e[(k - 1) * head:k * head, lanes] = replicate(start)

    for k in range(CHUNKS):
        rows = slice(k * head, (k + 1) * head)

        def solve(t, carry):
            value = offsets[t, k:k + 1, :] + jnp.sum(
                maps[t, rows, :] * spread_e[rows, :], axis=0, keepdims=True)
            full_view[k, pl.ds(t, 1), :] = value
            return carry

        lax.fori_loop(0, length, solve, 0, unroll=4)
    adj_ref[...] = full[...].astype(BF16)

    @pl.when(me > 0)
    def _():
        copy.wait_send()


def on_device(layer_inputs, states, cotangent, block_weights):
    tokens, units = states.shape
    heads, head, _ = block_weights.shape
    length = tokens // CHUNKS
    flat = jnp.transpose(block_weights, (1, 0, 2)).reshape(head, units)
    vmem = pl.BlockSpec(memory_space=pltpu.VMEM)
    adj = pl.pallas_call(
        recurrence,
        out_shape=jax.ShapeDtypeStruct((tokens, units), BF16),
        in_specs=[vmem] * 3,
        out_specs=vmem,
        scratch_shapes=[
            pltpu.VMEM((length, CHUNKS * head, units), F32),
            pltpu.VMEM((length, CHUNKS, units), F32),
            pltpu.VMEM((CHUNKS * head, units), F32),
            pltpu.VMEM((CHUNKS, units), F32),
            pltpu.VMEM((CHUNKS * head, units), F32),
            pltpu.VMEM((tokens, units), F32),
            pltpu.VMEM((1, units), F32),
            pltpu.VMEM((1, units), F32),
            pltpu.SemaphoreType.DMA,
            pltpu.SemaphoreType.DMA,
        ],
        compiler_params=pltpu.CompilerParams(
            collective_id=0, has_side_effects=True, vmem_limit_bytes=48 * 1024 * 1024),
    )(states, cotangent, flat)
    wide = lax.all_gather(layer_inputs, "tp", axis=1, tiled=True)
    mine = lax.all_to_all(wide, "ctx", split_axis=1, concat_axis=0, tiled=True)
    every = lax.all_gather(adj, "ctx", axis=0, tiled=True)
    block = lax.dot_general(mine, every, (((0,), (0,)), ((), ())), preferred_element_type=F32)
    return lax.all_to_all(block, "tp", split_axis=0, concat_axis=1, tiled=True)


def solution(mesh):
    in_specs = (P("ctx", "tp"), P("ctx", "tp"), P("ctx", "tp"), P("tp", None, None))
    out_specs = P(("ctx", "tp"), None)
    return jax.shard_map(
        on_device, mesh=mesh, in_specs=in_specs, out_specs=out_specs, check_vma=False
    )
```

time: 383 us -> 188 us (0.49); the launches traced: 376 us -> 188 us
  matrix products: 136 us -> 2.02 us
  waiting for transfers between devices: 125 us -> 6.16 us
  Pallas kernels: 0 us -> 110 us
  local copies, waits for them, and re-layouts: 65 us -> 4.14 us
  blocking collectives: 20 us -> 52.2 us
  starting transfers between devices: 9.06 us -> 0.01 us
  other arithmetic: 4.9 us -> 0 us
    dot_general x113 -> x1, matrix products: 136 us -> 2.02 us  [on_device(): lax.dot_general(mine, every, (((0,), (0,)), ((), ())), preferred_element_...]
    pallas_call x0 -> x1, Pallas kernels: none -> 110 us  [on_device(): pl.pallas_call(recurrence, out_shape=jax.ShapeDtypeStruct((tokens, units)...]
    reduce_scatter x1 -> x0, waiting for transfers between devices: 89.2 us -> none  [on_device(): lax.psum_scatter(lax.dot_general(gathered, adjoint_bf, (((0,), (1,)), (()...]
    ppermute x7 -> x0, waiting for transfers between devices: 35.7 us -> none  [from_behind(): return lax.ppermute(value, axis, pairs)]
    all_to_all x1 -> x2, blocking collectives: 11.4 us -> 43.6 us  [the longest x1 32.4 us: on_device(): mine = lax.all_to_all(wide, 'ctx', split_axis=1, concat_axis=0, tiled=True)]
    mul x32 -> x0, local copies, waits for them, and re-layouts: 24.5 us -> none  [build_step(): matrices = slope_now[..., None] * pulled]
    pad x6 -> x0, local copies, waits for them, and re-layouts: 17.5 us -> none  [on_device(): suffix = lax.associative_scan(compose, flipped, axis=2)]
    unnamed x14 -> x6, local copies, waits for them, and re-layouts: 11.5 us -> 1.99 us
  transfers between devices with their start and end apart: 8 -> 1, of which waited for: 8 -> 1; matrix products, arithmetic and copies ran while one was open for 0% -> 0% of each run, Pallas kernels for 0% -> 0%
where the time goes in v1:
time: 188 us
  Pallas kernels  110 us (59%)
  blocking collectives  52.2 us (28%)
  between operations  13.4 us (7%)
  waiting for transfers between devices  6.16 us (3%)
  local copies, waits for them, and re-layouts  4.14 us (2%)
  matrix products  2.02 us (1%)
    pallas_call x1, Pallas kernels, on_device(): pl.pallas_call(recurrence, out_shape=jax.ShapeDtypeStruct((tokens, units)...  110 us
    all_to_all x1, blocking collectives, on_device(): mine = lax.all_to_all(wide, 'ctx', split_axis=1, concat_axis=0, tiled=True)  32.4 us
    all_to_all x1, blocking collectives, on_device(): return lax.all_to_all(block, 'tp', split_axis=0, concat_axis=1, tiled=True)  11.2 us
    all_gather x1, blocking collectives, on_device(): wide = lax.all_gather(layer_inputs, 'tp', axis=1, tiled=True)  8.6 us
    all_gather x1, waiting for transfers between devices, on_device(): every = lax.all_gather(adj, 'ctx', axis=0, tiled=True)  6.15 us
  transfers between devices with their start and end apart: 1, of which 1 were waited for; matrix products, arithmetic and copies ran while one was open for 0% of the time, Pallas kernels for 0%

profile of v1, /device:TPU:0, one launch (start us, length us, event | category | flops | bytes accessed | tf_op | source)
XLA Modules:
  0.0 187.7 jit_solution(9336218874321134925)
XLA Ops:
  6.5 0.0 copy-start.2
  6.5 0.0 all-gather.2.cloned.1.call-start
  6.5 1.1 copy.12
  7.7 0.1 reshape.9.weights_ref
  7.8 0.0 copy-start
  7.8 1.0 copy-done
  8.8 0.0 copy-start.1
  8.8 1.0 copy-done.1
  9.8 109.7 %shard_map.46 = bf16[192,512]{1,0:T(8,128)(2,1)} custom-call(f32[192,512]{1,0:T(8,128)S(1)} %copy-done, f32[192,512]{1,0:T(8,128)S(1)} %copy-done.1, f32[64,512]{1,0:T(8,128)S(1)} %reshape.9.weights_ref), custom_call_target="tpu_custom_call" | custom-call | tf_op jit(solution)/shard_map/pallas_call | solution.py:174
  119.5 0.0 all-gather.2.cloned.1.call-update
  119.5 0.0 copy-done.2
  119.5 8.6 %all_gather.7 = bf16[192,2048]{1,0:T(8,128)(2,1)S(1)} all-gather(bf16[192,512]{1,0:T(8,128)(2,1)S(1)} %copy-done.2), channel_id=1, replica_groups=mesh['ctx'=8,'tp'=4] {'tp'}, dimensions={1}, use_global_device_ids=true | all-gather | bytes 983040 | tf_op jit(solution)/shard_map/all_gather | solution.py:194
  128.1 0.1 copy.18
  128.2 32.4 %all_to_all.38 = bf16[192,8,256]{2,0,1:T(8,128)(2,1)S(1)} all-to-all(bf16[192,8,256]{2,0,1:T(8,128)(2,1)S(1)} %bitcast.16), channel_id=1, replica_groups=mesh['ctx'=8,'tp'=4] {'ctx'}, dimensions={1} | all-to-all | bytes 1572864 | tf_op jit(solution)/shard_map/all_to_all | solution.py:195
  160.6 6.1 %all-gather.2.cloned.1.call-done = bf16[1536,512]{1,0:T(8,128)(2,1)} async-done(((bf16[192,512]{1,0:T(8,128)(2,1)}), bf16[1536,512]{1,0:T(8,128)(2,1)}) %all-gather.2.cloned.1.call-update) | async-done | bytes 1572880 | tf_op jit(solution)/shard_map/all_gather | solution.py:196
  166.7 2.0 %fusion = f32[512,256]{0,1:T(8,128)S(1)} fusion(bf16[1536,512]{1,0:T(8,128)(2,1)} %all-gather.2.cloned.1.call-done, bf16[1536,256]{1,0:T(8,128)(2,1)S(1)} %bitcast.19), kind=kOutput, calls=%fused_computation.1 | convolution fusion | flops 402653184 | bytes 2883584 | tf_op jit(solution)/shard_map/dot_general | solution.py:197
  168.7 11.2 %all_to_all.39 = f32[4,64,512]{2,1,0:T(8,128)S(1)} all-to-all(f32[4,64,512]{2,1,0:T(8,128)S(1)} %bitcast.20), channel_id=1, replica_groups=mesh['ctx'=8,'tp'=4] {'tp'}, dimensions={0} | all-to-all | bytes 1048576 | tf_op jit(solution)/shard_map/all_to_all | solution.py:198
  180.0 0.8 copy.16
Async XLA Ops:
  6.5 113.0 %copy-start.2 = (bf16[192,512]{1,0:T(8,128)(2,1)S(1)}, bf16[192,512]{1,0:T(8,128)(2,1)}, u32[]{:S(2)}) copy-start(bf16[192,512]{1,0:T(8,128)(2,1)} %param.4) | copy-start | bytes 589828
  6.5 160.2 %all-gather.2.cloned.1.call-start = ((), (), s32[]{:S(2)}) async-start(), calls=%async_computation.2 | async-start | bytes 1769472 | tf_op jit(solution)/shard_map/all_gather | solution.py:196
  7.8 1.0 copy-start
  8.8 1.0 copy-start.1
Sparse Core Ops, SparseCore 0:
  119.6 47.0 all-gather.1

commit v2 on v1

v2 whole, which is shorter than its diff:
```python
import jax
import jax.numpy as jnp
from jax import lax
from jax.experimental import pallas as pl
from jax.experimental.pallas import tpu as pltpu
from jax.sharding import PartitionSpec as P

MESH = pl.DeviceIdType.MESH
CHUNKS = 8
PAD = 16
F32 = jnp.float32
BF16 = jnp.bfloat16


def halves(value):
    high = value.astype(BF16)
    low = (value - high.astype(F32)).astype(BF16)
    return high, low


def dot(left, right):
    return jnp.dot(left, right, preferred_element_type=F32)


def left_terms(value):
    high, low = halves(value)
    return jnp.concatenate([high, low, high], axis=1)


def right_terms(value):
    high, low = halves(value)
    return jnp.concatenate([high, high, low], axis=0)


def recurrence(states_ref, cot_ref, weights_ref, pieces_ref, adj_ref, mine_ref,
               maps, weights, suffix, suffix_vec, spread_e, full, e_in, e_out,
               send_sem, recv_sem, local_sem, piece_send, piece_recv):
    n = lax.axis_size("ctx")
    ranks = lax.axis_size("tp")
    me = lax.axis_index("ctx")
    rank = lax.axis_index("tp")
    tokens, units = states_ref.shape
    head = weights_ref.shape[0]
    length = tokens // CHUNKS
    width = min(256, units)
    groups = units // width
    tile = width // head
    rows_all = CHUNKS * head
    pieces = pieces_ref.shape[0]
    last = length - 1

    barrier = pltpu.get_barrier_semaphore()
    pl.semaphore_signal(barrier, inc=1, device_id={"ctx": lax.rem(me + 1, n)}, device_id_type=MESH)
    pl.semaphore_signal(barrier, inc=1, device_id={"ctx": lax.rem(me + n - 1, n)}, device_id_type=MESH)
    source_rank = me // pieces
    own = source_rank == rank
    for c in range(n):
        @pl.when(jnp.logical_not(jnp.logical_and(own, me == c)))
        def _():
            pl.semaphore_signal(barrier, inc=1, device_id={"ctx": c, "tp": source_rank},
                                device_id_type=MESH)
    pl.semaphore_wait(barrier, 2 + pieces * ranks - own.astype(jnp.int32))

    def piece_copy(p, t):
        return pltpu.make_async_remote_copy(
            src_ref=pieces_ref.at[p], dst_ref=mine_ref.at[me],
            send_sem=piece_send.at[p * ranks + t], recv_sem=piece_recv.at[me],
            device_id={"ctx": rank * pieces + p, "tp": t}, device_id_type=MESH)

    own_piece = lax.max(me - rank * pieces, 0)
    local = pltpu.make_async_copy(
        pieces_ref.at[lax.min(own_piece, pieces - 1)], mine_ref.at[me], local_sem)

    def to_other(p, t):
        return jnp.logical_not(jnp.logical_and(rank * pieces + p == me, rank == t))

    for p in range(pieces):
        for t in range(ranks):
            @pl.when(to_other(p, t))
            def _():
                piece_copy(p, t).start()

    @pl.when(own)
    def _():
        local.start()

    mask = (lax.broadcasted_iota(jnp.int32, (width, width), 0) // head
            == lax.broadcasted_iota(jnp.int32, (width, width), 1) // head)

    def spread(rows):
        return right_terms(jnp.where(mask, jnp.concatenate([rows] * tile, axis=0), 0.0))

    for g in range(groups):
        weights[g] = spread(weights_ref[:, g * width:(g + 1) * width])

    states_view = states_ref.reshape(CHUNKS, length, units)
    cot_view = cot_ref.reshape(CHUNKS, length, units)
    full_view = full.reshape(CHUNKS, length, units)
    blank = jnp.zeros((PAD - CHUNKS, units), F32)

    def token_rows(ref, t):
        return jnp.concatenate([ref[k, pl.ds(t, 1), :] for k in range(CHUNKS)] + [blank], axis=0)

    def slopes_at(t):
        h = token_rows(states_view, t)
        return 1.0 - h * h

    s_last = slopes_at(last)
    maps[last, rows_all:, :] = s_last * token_rows(cot_view, last)
    for k in range(CHUNKS):
        maps[last, k * head:(k + 1) * head, :] = weights_ref[...] * s_last[k:k + 1, :]

    def step(i, carry):
        t = last - 1 - i
        s = slopes_at(t)
        c = token_rows(cot_view, t)
        for g in range(groups):
            lanes = slice(g * width, (g + 1) * width)
            y = dot(left_terms(maps[t + 1, :, lanes]), weights[g])
            for k in range(CHUNKS):
                rows = slice(k * head, (k + 1) * head)
                maps[t, rows, lanes] = y[rows] * s[k:k + 1, lanes]
            maps[t, rows_all:, lanes] = s[:, lanes] * (c[:, lanes] + y[rows_all:])
        return carry

    lax.fori_loop(0, last, step, 0)

    state = [None] * groups
    for k in range(CHUNKS - 1, -1, -1):
        rows = slice(k * head, (k + 1) * head)
        for g in range(groups):
            lanes = slice(g * width, (g + 1) * width)
            vec = maps[0, rows_all + k:rows_all + k + 1, lanes]
            if k == CHUNKS - 1:
                running = maps[0, rows, lanes]
            else:
                y = dot(left_terms(state[g]), spread(maps[0, rows, lanes]))
                running = y[:head]
                vec = vec + y[head:head + 1]
            state[g] = jnp.concatenate([running, jnp.broadcast_to(vec, (PAD, width))], axis=0)
            suffix[rows, lanes] = running
            suffix_vec[k:k + 1, lanes] = vec

    ones = mask.astype(F32).astype(BF16)
    ones2 = jnp.concatenate([ones, ones], axis=0)
    pick = (lax.broadcasted_iota(jnp.int32, (head, width), 1) % head
            == lax.broadcasted_iota(jnp.int32, (head, width), 0))

    def marked(row):
        high, low = halves(jnp.where(pick, jnp.broadcast_to(row, (head, width)), 0.0))
        return jnp.concatenate([high, low], axis=1)

    copy = pltpu.make_async_remote_copy(
        src_ref=e_out, dst_ref=e_in, send_sem=send_sem, recv_sem=recv_sem,
        device_id={"ctx": lax.max(me - 1, 0)}, device_id_type=MESH)

    @pl.when(me == n - 1)
    def _():
        e_in[...] = jnp.zeros_like(e_in)

    @pl.when(me < n - 1)
    def _():
        copy.wait_recv()

    spreads = []
    for g in range(groups):
        lanes = slice(g * width, (g + 1) * width)
        e = dot(marked(e_in[:, lanes]), ones2)
        spreads.append(e)
        e_out[:, lanes] = suffix_vec[0:1, lanes] + jnp.sum(
            e * suffix[0:head, lanes], axis=0, keepdims=True)

    @pl.when(me > 0)
    def _():
        copy.start()

    for g in range(groups):
        lanes = slice(g * width, (g + 1) * width)
        e = spreads[g]
        starts = [marked(suffix_vec[k:k + 1, lanes] + jnp.sum(
            e * suffix[k * head:(k + 1) * head, lanes], axis=0, keepdims=True))
            for k in range(1, CHUNKS)]
        spread_e[:rows_all - head, lanes] = dot(jnp.concatenate(starts, axis=0), ones2)
        spread_e[rows_all - head:, lanes] = e

    for k in range(CHUNKS):
        for g in range(groups):
            rows = slice(k * head, (k + 1) * head)
            lanes = slice(g * width, (g + 1) * width)
            e = spread_e[rows, lanes]

            def solve(t, carry):
                value = maps[t, rows_all + k:rows_all + k + 1, lanes] + jnp.sum(
                    maps[t, rows, lanes] * e, axis=0, keepdims=True)
                full_view[k, pl.ds(t, 1), lanes] = value
                return carry

            lax.fori_loop(0, length, solve, 0, unroll=8)
    adj_ref[...] = full[...].astype(BF16)

    @pl.when(me > 0)
    def _():
        copy.wait_send()

    for p in range(pieces):
        for t in range(ranks):
            @pl.when(to_other(p, t))
            def _():
                piece_copy(p, t).wait_send()
    for c in range(n):
        @pl.when(jnp.logical_not(jnp.logical_and(own, me == c)))
        def _():
            pltpu.make_async_remote_copy(
                src_ref=pieces_ref.at[0], dst_ref=mine_ref.at[c],
                send_sem=piece_send.at[0], recv_sem=piece_recv.at[c],
                device_id={"ctx": c, "tp": source_rank}, device_id_type=MESH).wait_recv()

    @pl.when(own)
    def _():
        local.wait()


def on_device(layer_inputs, states, cotangent, block_weights):
    tokens, units = states.shape
    heads, head, _ = block_weights.shape
    n = lax.axis_size("ctx")
    ranks = lax.axis_size("tp")
    features = layer_inputs.shape[1]
    columns = features * ranks // n
    pieces = features // columns
    length = tokens // CHUNKS
    width = min(256, units)
    flat = jnp.transpose(block_weights, (1, 0, 2)).reshape(head, units)
    cut = jnp.transpose(layer_inputs.reshape(tokens, pieces, columns), (1, 0, 2))
    vmem = pl.BlockSpec(memory_space=pltpu.VMEM)
    hbm = pl.BlockSpec(memory_space=pl.ANY)
    adj, mine = pl.pallas_call(
        recurrence,
        out_shape=(jax.ShapeDtypeStruct((tokens, units), BF16),
                   jax.ShapeDtypeStruct((n, tokens, columns), BF16)),
        in_specs=[vmem] * 3 + [hbm],
        out_specs=(vmem, hbm),
        scratch_shapes=[
            pltpu.VMEM((length, CHUNKS * head + PAD, units), F32),
            pltpu.VMEM((units // width, 3 * width, width), BF16),
            pltpu.VMEM((CHUNKS * head, units), F32),
            pltpu.VMEM((CHUNKS, units), F32),
            pltpu.VMEM((CHUNKS * head, units), F32),
            pltpu.VMEM((tokens, units), F32),
            pltpu.VMEM((1, units), F32),
            pltpu.VMEM((1, units), F32),
            pltpu.SemaphoreType.DMA,
            pltpu.SemaphoreType.DMA,
            pltpu.SemaphoreType.DMA,
            pltpu.SemaphoreType.DMA((pieces * ranks,)),
            pltpu.SemaphoreType.DMA((n,)),
        ],
        compiler_params=pltpu.CompilerParams(
            collective_id=0, has_side_effects=True, vmem_limit_bytes=48 * 1024 * 1024),
    )(states, cotangent, flat, cut)
    every = lax.all_gather(adj, "ctx", axis=0, tiled=True)
    mine = mine.reshape(n * tokens, columns)
    block = lax.dot_general(mine, every, (((0,), (0,)), ((), ())), preferred_element_type=F32)
    return lax.all_to_all(block, "tp", split_axis=0, concat_axis=1, tiled=True)


def solution(mesh):
    in_specs = (P("ctx", "tp"), P("ctx", "tp"), P("ctx", "tp"), P("tp", None, None))
    out_specs = P(("ctx", "tp"), None)
    return jax.shard_map(
        on_device, mesh=mesh, in_specs=in_specs, out_specs=out_specs, check_vma=False
    )
```

time: 188 us -> 128 us (0.68)
  Pallas kernels: 110 us -> 57.4 us
  blocking collectives: 52.2 us -> 11.4 us
  waiting for transfers between devices: 6.16 us -> 40.6 us
    pallas_call x1, Pallas kernels: 110 us -> 57.4 us  [on_device(): pl.pallas_call(recurrence, out_shape=(jax.ShapeDtypeStruct((tokens, units...]
    all_gather x1, waiting for transfers between devices: 6.15 us -> 40.6 us  [on_device(): every = lax.all_gather(adj, 'ctx', axis=0, tiled=True)]
    all_to_all x1 -> x0, blocking collectives: 32.4 us -> none  [on_device(): mine = lax.all_to_all(wide, 'ctx', split_axis=1, concat_axis=0, tiled=True)]
    all_gather x1 -> x0, blocking collectives: 8.6 us -> none  [on_device(): wide = lax.all_gather(layer_inputs, 'tp', axis=1, tiled=True)]
    unnamed x6 -> x4, local copies, waits for them, and re-layouts: 1.99 us -> 0.01 us
where the time goes in v2:
time: 128 us
  Pallas kernels  57.4 us (45%)
  waiting for transfers between devices  40.6 us (32%)
  between operations  13.4 us (10%)
  blocking collectives  11.4 us (9%)
  local copies, waits for them, and re-layouts  3.36 us (3%)
  matrix products  1.97 us (2%)
    pallas_call x1, Pallas kernels, on_device(): pl.pallas_call(recurrence, out_shape=(jax.ShapeDtypeStruct((tokens, units...  57.4 us
    all_gather x1, waiting for transfers between devices, on_device(): every = lax.all_gather(adj, 'ctx', axis=0, tiled=True)  40.6 us
    all_to_all x1, blocking collectives, on_device(): return lax.all_to_all(block, 'tp', split_axis=0, concat_axis=1, tiled=True)  11.4 us
  transfers between devices with their start and end apart: 1, of which 1 were waited for; matrix products, arithmetic and copies ran while one was open for 0% of the time, Pallas kernels for 0%

profile of v2, /device:TPU:0, one launch (start us, length us, event | category | flops | bytes accessed | tf_op | source)
XLA Modules:
  0.0 128.2 jit_solution(17722191875134524569)
XLA Ops:
  6.5 0.0 copy-start.1
  6.5 0.0 copy-start
  6.5 0.0 all-gather.2.cloned.1.call-start
  6.5 1.0 copy.14
  7.6 1.1 copy.7
  8.7 0.1 reshape.13.weights_ref
  8.8 0.0 copy-done.1
  8.8 0.0 copy-done
  8.8 57.4 %shard_map.46 = (bf16[192,512]{1,0:T(8,128)(2,1)}, bf16[8,192,256]{2,1,0:T(8,128)(2,1)S(1)}) custom-call(f32[192,512]{1,0:T(8,128)S(1)} %copy-done, f32[192,512]{1,0:T(8,128)S(1)} %copy-done.1, f32[64,512]{1,0:T(8,128)S(1)} %reshape.13.weights_ref, bf16[2,192,256]{2,1,0:T(8,128)(2,1)S(1)} %bitcast.20), custom_call_target="tpu_custom_call" | custom-call | tf_op jit(solution)/shard_map/pallas_call | solution.py:237
  66.2 0.0 all-gather.2.cloned.1.call-update
  66.3 0.3 copy.9
  66.5 40.6 %all-gather.2.cloned.1.call-done = bf16[1536,512]{1,0:T(8,128)(2,1)} async-done(((bf16[192,512]{1,0:T(8,128)(2,1)}), bf16[1536,512]{1,0:T(8,128)(2,1)}) %all-gather.2.cloned.1.call-update) | async-done | bytes 1572880 | tf_op jit(solution)/shard_map/all_gather | solution.py:261
  107.2 2.0 %fusion = f32[4,64,512]{2,1,0:T(8,128)S(1)} fusion(bf16[4,64,1536]{2,1,0:T(8,128)(2,1)S(1)} %bitcast.21, bf16[1536,512]{1,0:T(8,128)(2,1)} %all-gather.2.cloned.1.call-done), kind=kOutput, calls=%fused_computation | convolution fusion | flops 402653184 | bytes 2883584 | tf_op jit(solution)/shard_map/dot_general | solution.py:263
  109.1 11.4 %all_to_all.16 = f32[4,64,512]{2,1,0:T(8,128)S(1)} all-to-all(f32[4,64,512]{2,1,0:T(8,128)S(1)} %fusion), channel_id=1, replica_groups=mesh['ctx'=8,'tp'=4] {'tp'}, dimensions={0} | all-to-all | bytes 1048576 | tf_op jit(solution)/shard_map/all_to_all | solution.py:264
  120.5 0.8 copy.12
Async XLA Ops:
  6.5 2.3 %copy-start.1 = (f32[192,512]{1,0:T(8,128)S(1)}, f32[192,512]{1,0:T(8,128)}, u32[]{:S(2)}) copy-start(f32[192,512]{1,0:T(8,128)} %cot_ref.1) | copy-start | bytes 1179652
  6.5 2.3 %copy-start = (f32[192,512]{1,0:T(8,128)S(1)}, f32[192,512]{1,0:T(8,128)}, u32[]{:S(2)}) copy-start(f32[192,512]{1,0:T(8,128)} %states_ref.1) | copy-start | bytes 1179652
  6.5 100.6 %all-gather.2.cloned.1.call-start = ((), (), s32[]{:S(2)}) async-start(), calls=%async_computation.1 | async-start | bytes 1769472 | tf_op jit(solution)/shard_map/all_gather | solution.py:261
Sparse Core Ops, SparseCore 0:
  66.4 40.7 all-gather.1

commit v3 on v2

--- a/solution.py
+++ b/solution.py
@@ -32,9 +32,10 @@
     return jnp.concatenate([high, high, low], axis=0)
 
 
-def recurrence(states_ref, cot_ref, weights_ref, pieces_ref, adj_ref, mine_ref,
-               maps, weights, suffix, suffix_vec, spread_e, full, e_in, e_out,
-               send_sem, recv_sem, local_sem, piece_send, piece_recv):
+def backward(states_ref, cot_ref, weights_ref, pieces_ref, out_ref,
+             maps, weights, relay_weights, suffix, suffix_vec, spread_e, full, mine_ref, blocks,
+             total, e_in, e_out, send_sem, recv_sem, local_sem, piece_send, piece_recv,
+             line_send, pair_send, block_recv, rows_send, rows_recv):
     n = lax.axis_size("ctx")
     ranks = lax.axis_size("tp")
     me = lax.axis_index("ctx")
@@ -48,6 +49,7 @@
     rows_all = CHUNKS * head
     pieces = pieces_ref.shape[0]
     last = length - 1
+    outer = n // 2
 
     barrier = pltpu.get_barrier_semaphore()
     pl.semaphore_signal(barrier, inc=1, device_id={"ctx": lax.rem(me + 1, n)}, device_id_type=MESH)
@@ -59,7 +61,16 @@
         def _():
             pl.semaphore_signal(barrier, inc=1, device_id={"ctx": c, "tp": source_rank},
                                 device_id_type=MESH)
-    pl.semaphore_wait(barrier, 2 + pieces * ranks - own.astype(jnp.int32))
+    across = me + 1 - 2 * lax.rem(me, 2)
+    pl.semaphore_signal(barrier, inc=1, device_id={"ctx": across}, device_id_type=MESH)
+    for k in range(1, outer):
+        pl.semaphore_signal(barrier, inc=1, device_id={"ctx": lax.rem(me + 2 * k, n)},
+                            device_id_type=MESH)
+    for k in range(1, ranks):
+        pl.semaphore_signal(barrier, inc=1, device_id={"tp": lax.rem(rank + k, ranks)},
+                            device_id_type=MESH)
+    pl.semaphore_wait(
+        barrier, 2 + 1 + outer - 1 + ranks - 1 + pieces * ranks - own.astype(jnp.int32))
 
     def piece_copy(p, t):
         return pltpu.make_async_remote_copy(
@@ -150,6 +161,9 @@
         high, low = halves(jnp.where(pick, jnp.broadcast_to(row, (head, width)), 0.0))
         return jnp.concatenate([high, low], axis=1)
 
+    for g in range(groups):
+        relay_weights[g] = spread(suffix[0:head, g * width:(g + 1) * width])
+
     copy = pltpu.make_async_remote_copy(
         src_ref=e_out, dst_ref=e_in, send_sem=send_sem, recv_sem=recv_sem,
         device_id={"ctx": lax.max(me - 1, 0)}, device_id_type=MESH)
@@ -162,31 +176,48 @@
     def _():
         copy.wait_recv()
 
-    spreads = []
+    for g in range(groups):
+        lanes = slice(g * width, (g + 1) * width)
+        e = jnp.broadcast_to(e_in[:, lanes], (PAD, width))
+        e_out[:, lanes] = suffix_vec[0:1, lanes] + dot(left_terms(e), relay_weights[g])[0:1]
+
+    @pl.when(me > 0)
+    def _():
+        copy.start()
+
     for g in range(groups):
         lanes = slice(g * width, (g + 1) * width)
         e = dot(marked(e_in[:, lanes]), ones2)
-        spreads.append(e)
-        e_out[:, lanes] = suffix_vec[0:1, lanes] + jnp.sum(
-            e * suffix[0:head, lanes], axis=0, keepdims=True)
-
-    @pl.when(me > 0)
-    def _():
-        copy.start()
-
-    for g in range(groups):
-        lanes = slice(g * width, (g + 1) * width)
-        e = spreads[g]
         starts = [marked(suffix_vec[k:k + 1, lanes] + jnp.sum(
             e * suffix[k * head:(k + 1) * head, lanes], axis=0, keepdims=True))
             for k in range(1, CHUNKS)]
         spread_e[:rows_all - head, lanes] = dot(jnp.concatenate(starts, axis=0), ones2)
         spread_e[rows_all - head:, lanes] = e
 
-    for k in range(CHUNKS):
-        for g in range(groups):
+    def line_copy(g, o):
+        return pltpu.make_async_remote_copy(
+            src_ref=blocks.at[me, g], dst_ref=blocks.at[me, g],
+            send_sem=line_send.at[g, o], recv_sem=block_recv.at[me, g],
+            device_id={"ctx": 2 * o + lax.rem(me, 2)}, device_id_type=MESH)
+
+    def pair_copy(g, o):
+        c = 2 * o + lax.rem(me, 2)
+        return pltpu.make_async_remote_copy(
+            src_ref=blocks.at[c, g], dst_ref=blocks.at[c, g],
+            send_sem=pair_send.at[g, o], recv_sem=block_recv.at[c, g],
+            device_id={"ctx": across}, device_id_type=MESH)
+
+    def arrived(c, g):
+        pltpu.make_async_remote_copy(
+            src_ref=blocks.at[c, g], dst_ref=blocks.at[c, g],
+            send_sem=line_send.at[g, 0], recv_sem=block_recv.at[c, g],
+            device_id={"ctx": across}, device_id_type=MESH).wait_recv()
+
+    place = me // 2
+    for g in range(groups):
+        lanes = slice(g * width, (g + 1) * width)
+        for k in range(CHUNKS):
             rows = slice(k * head, (k + 1) * head)
-            lanes = slice(g * width, (g + 1) * width)
             e = spread_e[rows, lanes]
 
             def solve(t, carry):
@@ -196,17 +227,21 @@
                 return carry
 
             lax.fori_loop(0, length, solve, 0, unroll=8)
-    adj_ref[...] = full[...].astype(BF16)
-
-    @pl.when(me > 0)
-    def _():
-        copy.wait_send()
-
-    for p in range(pieces):
-        for t in range(ranks):
-            @pl.when(to_other(p, t))
+        blocks[me, g] = full[:, lanes].astype(BF16)
+        pair_copy(g, place).start()
+
+        def send(o, carry):
+            @pl.when(o != place)
             def _():
-                piece_copy(p, t).wait_send()
+                line_copy(g, o).start()
+            return carry
+
+        lax.fori_loop(0, outer, send, 0)
+
+    @pl.when(own)
+    def _():
+        local.wait()
+
     for c in range(n):
         @pl.when(jnp.logical_not(jnp.logical_and(own, me == c)))
         def _():
@@ -215,9 +250,67 @@
                 send_sem=piece_send.at[0], recv_sem=piece_recv.at[c],
                 device_id={"ctx": c, "tp": source_rank}, device_id_type=MESH).wait_recv()
 
-    @pl.when(own)
-    def _():
-        local.wait()
+    total[...] = jnp.zeros_like(total)
+
+    def gather(i, carry):
+        o = outer - 1 - i
+        near = 2 * o + lax.rem(me, 2)
+        far = 2 * o + 1 - lax.rem(me, 2)
+
+        @pl.when(o != place)
+        def _():
+            for g in range(groups):
+                arrived(near, g)
+                pair_copy(g, o).start()
+
+        for c in (near, far):
+            for g in range(groups):
+                lanes = slice(g * width, (g + 1) * width)
+                if c is far:
+                    arrived(far, g)
+                total[:, lanes] += dot(mine_ref[c], blocks[c, g])
+        return carry
+
+    lax.fori_loop(0, outer, gather, 0)
+
+    share = total.shape[0] // ranks
+
+    def rows_copy(t, source):
+        return pltpu.make_async_remote_copy(
+            src_ref=total.at[pl.ds(t * share, share)],
+            dst_ref=out_ref.at[:, pl.ds(pl.multiple_of(source * units, 128), units)],
+            send_sem=rows_send.at[t], recv_sem=rows_recv.at[source],
+            device_id={"tp": t}, device_id_type=MESH)
+
+    for k in range(1, ranks):
+        rows_copy(lax.rem(rank + k, ranks), rank).start()
+    out_ref[:, pl.ds(pl.multiple_of(rank * units, 128), units)] = total[
+        pl.ds(pl.multiple_of(rank * share, 8), share), :]
+
+    @pl.when(me > 0)
+    def _():
+        copy.wait_send()
+
+    for p in range(pieces):
+        for t in range(ranks):
+            @pl.when(to_other(p, t))
+            def _():
+                piece_copy(p, t).wait_send()
+
+    def drain(o, carry):
+        for g in range(groups):
+            pair_copy(g, o).wait_send()
+
+            @pl.when(o != place)
+            def _():
+                line_copy(g, o).wait_send()
+        return carry
+
+    lax.fori_loop(0, outer, drain, 0)
+    for k in range(1, ranks):
+        t = lax.rem(rank + k, ranks)
+        rows_copy(t, t).wait_recv()
+        rows_copy(t, rank).wait_send()
 
 
 def on_device(layer_inputs, states, cotangent, block_weights):
@@ -231,22 +324,25 @@
     length = tokens // CHUNKS
     width = min(256, units)
     flat = jnp.transpose(block_weights, (1, 0, 2)).reshape(head, units)
-    cut = jnp.transpose(layer_inputs.reshape(tokens, pieces, columns), (1, 0, 2))
+    cut = jnp.transpose(layer_inputs).reshape(pieces, columns, tokens)
+    groups = units // width
     vmem = pl.BlockSpec(memory_space=pltpu.VMEM)
-    hbm = pl.BlockSpec(memory_space=pl.ANY)
-    adj, mine = pl.pallas_call(
-        recurrence,
-        out_shape=(jax.ShapeDtypeStruct((tokens, units), BF16),
-                   jax.ShapeDtypeStruct((n, tokens, columns), BF16)),
-        in_specs=[vmem] * 3 + [hbm],
-        out_specs=(vmem, hbm),
+    return pl.pallas_call(
+        backward,
+        out_shape=jax.ShapeDtypeStruct((columns // ranks, units * ranks), F32),
+        in_specs=[vmem] * 4,
+        out_specs=vmem,
         scratch_shapes=[
             pltpu.VMEM((length, CHUNKS * head + PAD, units), F32),
-            pltpu.VMEM((units // width, 3 * width, width), BF16),
+            pltpu.VMEM((groups, 3 * width, width), BF16),
+            pltpu.VMEM((groups, 3 * width, width), BF16),
             pltpu.VMEM((CHUNKS * head, units), F32),
             pltpu.VMEM((CHUNKS, units), F32),
             pltpu.VMEM((CHUNKS * head, units), F32),
             pltpu.VMEM((tokens, units), F32),
+            pltpu.VMEM((n, columns, tokens), BF16),
+            pltpu.VMEM((n, groups, tokens, width), BF16),
+            pltpu.VMEM((columns, units), F32),
             pltpu.VMEM((1, units), F32),
             pltpu.VMEM((1, units), F32),
             pltpu.SemaphoreType.DMA,
@@ -254,14 +350,15 @@
             pltpu.SemaphoreType.DMA,
             pltpu.SemaphoreType.DMA((pieces * ranks,)),
             pltpu.SemaphoreType.DMA((n,)),
+            pltpu.SemaphoreType.DMA((groups, n // 2)),
+            pltpu.SemaphoreType.DMA((groups, n // 2)),
+            pltpu.SemaphoreType.DMA((n, groups)),
+            pltpu.SemaphoreType.DMA((ranks,)),
+            pltpu.SemaphoreType.DMA((ranks,)),
         ],
         compiler_params=pltpu.CompilerParams(
             collective_id=0, has_side_effects=True, vmem_limit_bytes=48 * 1024 * 1024),
     )(states, cotangent, flat, cut)
-    every = lax.all_gather(adj, "ctx", axis=0, tiled=True)
-    mine = mine.reshape(n * tokens, columns)
-    block = lax.dot_general(mine, every, (((0,), (0,)), ((), ())), preferred_element_type=F32)
-    return lax.all_to_all(block, "tp", split_axis=0, concat_axis=1, tiled=True)
 
 
 def solution(mesh):

time: 128 us -> 99.6 us (0.78); the launches traced: 128 us -> 98.4 us
  waiting for transfers between devices: 40.6 us -> 0 us
  Pallas kernels: 57.4 us -> 95.4 us
  between operations: 13.4 us -> 0.05 us
  blocking collectives: 11.4 us -> 0 us
  matrix products: 1.97 us -> 0 us
    all_gather x1 -> x0, waiting for transfers between devices: 40.6 us -> none  [on_device(): every = lax.all_gather(adj, 'ctx', axis=0, tiled=True)]
    pallas_call x1, Pallas kernels: 57.4 us -> 95.4 us  [on_device(): pl.pallas_call(backward, out_shape=jax.ShapeDtypeStruct((columns // ranks...]
    all_to_all x1 -> x0, blocking collectives: 11.4 us -> none  [on_device(): return lax.all_to_all(block, 'tp', split_axis=0, concat_axis=1, tiled=True)]
    dot_general x1 -> x0, matrix products: 1.97 us -> none  [on_device(): lax.dot_general(mine, every, (((0,), (0,)), ((), ())), preferred_element_...]
    unnamed x4 -> x7, local copies, waits for them, and re-layouts: 0.01 us -> 1.62 us
  transfers between devices with their start and end apart: 1 -> 0, of which waited for: 1 -> 0; matrix products, arithmetic and copies ran while one was open for 0% -> 0% of each run, Pallas kernels for 0% -> 0%
where the time goes in v3:
time: 99.6 us; the launch traced here: 98.4 us
  Pallas kernels  95.4 us (96%)
  local copies, waits for them, and re-layouts  3 us (3%)
    pallas_call x1, Pallas kernels, on_device(): pl.pallas_call(backward, out_shape=jax.ShapeDtypeStruct((columns // ranks...  95.4 us

profile of v3, /device:TPU:0, one launch (start us, length us, event | category | flops | bytes accessed | tf_op | source)
XLA Modules:
  0.0 98.4 jit_solution(12249521976293900037)
XLA Ops:
  0.0 0.0 copy-start.2
  0.0 1.1 %copy.6 = bf16[512,192]{1,0:T(8,128)(2,1)S(1)} copy(bf16[512,192]{0,1:T(8,128)(2,1)} %bitcast.5) | data formatting | bytes 393216 | tf_op jit(solution)/shard_map/transpose | solution.py:327
  1.1 0.0 copy-done.2
  1.1 0.0 copy-start
  1.1 0.0 copy-start.1
  1.1 0.2 copy.5
  1.3 0.1 reshape.6.weights_ref
  1.4 0.7 copy-done
  2.1 0.1 copy-done.1
  2.2 95.4 %shard_map.46 = f32[64,2048]{1,0:T(8,128)S(1)} custom-call(f32[192,512]{1,0:T(8,128)S(1)} %copy-done, f32[192,512]{1,0:T(8,128)S(1)} %copy-done.1, f32[64,512]{1,0:T(8,128)S(1)} %reshape.6.weights_ref, bf16[2,256,192]{2,1,0:T(8,128)(2,1)S(1)} %bitcast.3), custom_call_target="tpu_custom_call" | custom-call | tf_op jit(solution)/shard_map/pallas_call | solution.py:330
  97.6 0.8 copy.8
Async XLA Ops:
  0.0 1.1 %copy-start.2 = (f32[8,64,64]{2,1,0:T(8,128)S(1)}, f32[8,64,64]{2,1,0:T(8,128)}, u32[]{:S(2)}) copy-start(f32[8,64,64]{2,1,0:T(8,128)} %param.7) | copy-start | bytes 393220
  1.1 1.0 %copy-start = (f32[192,512]{1,0:T(8,128)S(1)}, f32[192,512]{1,0:T(8,128)}, u32[]{:S(2)}) copy-start(f32[192,512]{1,0:T(8,128)} %states_ref.1) | copy-start | bytes 1179652
  1.1 1.1 %copy-start.1 = (f32[192,512]{1,0:T(8,128)S(1)}, f32[192,512]{1,0:T(8,128)}, u32[]{:S(2)}) copy-start(f32[192,512]{1,0:T(8,128)} %cot_ref.1) | copy-start | bytes 1179652

commit v4 on v3

--- a/solution.py
+++ b/solution.py
@@ -35,7 +35,7 @@
 def backward(states_ref, cot_ref, weights_ref, pieces_ref, out_ref,
              maps, weights, relay_weights, suffix, suffix_vec, spread_e, full, mine_ref, blocks,
              total, e_in, e_out, send_sem, recv_sem, local_sem, piece_send, piece_recv,
-             line_send, pair_send, block_recv, rows_send, rows_recv):
+             mine_send, mine_recv, line_send, pair_send, block_recv, rows_send, rows_recv):
     n = lax.axis_size("ctx")
     ranks = lax.axis_size("tp")
     me = lax.axis_index("ctx")
@@ -54,12 +54,12 @@
     barrier = pltpu.get_barrier_semaphore()
     pl.semaphore_signal(barrier, inc=1, device_id={"ctx": lax.rem(me + 1, n)}, device_id_type=MESH)
     pl.semaphore_signal(barrier, inc=1, device_id={"ctx": lax.rem(me + n - 1, n)}, device_id_type=MESH)
-    source_rank = me // pieces
-    own = source_rank == rank
-    for c in range(n):
-        @pl.when(jnp.logical_not(jnp.logical_and(own, me == c)))
-        def _():
-            pl.semaphore_signal(barrier, inc=1, device_id={"ctx": c, "tp": source_rank},
+    own = me // pieces == rank
+
+    @pl.when(own)
+    def _():
+        for k in range(1, n):
+            pl.semaphore_signal(barrier, inc=1, device_id={"ctx": lax.rem(me + k, n)},
                                 device_id_type=MESH)
     across = me + 1 - 2 * lax.rem(me, 2)
     pl.semaphore_signal(barrier, inc=1, device_id={"ctx": across}, device_id_type=MESH)
@@ -70,30 +70,32 @@
         pl.semaphore_signal(barrier, inc=1, device_id={"tp": lax.rem(rank + k, ranks)},
                             device_id_type=MESH)
     pl.semaphore_wait(
-        barrier, 2 + 1 + outer - 1 + ranks - 1 + pieces * ranks - own.astype(jnp.int32))
-
-    def piece_copy(p, t):
+        barrier, 2 + 1 + outer - 1 + ranks - 1 + pieces - own.astype(jnp.int32))
+
+    def piece_copy(p):
         return pltpu.make_async_remote_copy(
             src_ref=pieces_ref.at[p], dst_ref=mine_ref.at[me],
-            send_sem=piece_send.at[p * ranks + t], recv_sem=piece_recv.at[me],
-            device_id={"ctx": rank * pieces + p, "tp": t}, device_id_type=MESH)
+            send_sem=piece_send.at[p], recv_sem=piece_recv.at[me],
+            device_id={"ctx": rank * pieces + p}, device_id_type=MESH)
 
     own_piece = lax.max(me - rank * pieces, 0)
     local = pltpu.make_async_copy(
         pieces_ref.at[lax.min(own_piece, pieces - 1)], mine_ref.at[me], local_sem)
 
-    def to_other(p, t):
-        return jnp.logical_not(jnp.logical_and(rank * pieces + p == me, rank == t))
-
     for p in range(pieces):
-        for t in range(ranks):
-            @pl.when(to_other(p, t))
-            def _():
-                piece_copy(p, t).start()
+        @pl.when(rank * pieces + p != me)
+        def _():
+            piece_copy(p).start()
 
     @pl.when(own)
     def _():
         local.start()
+
+    def mine_copy(k):
+        return pltpu.make_async_remote_copy(
+            src_ref=mine_ref, dst_ref=mine_ref,
+            send_sem=mine_send.at[k], recv_sem=mine_recv,
+            device_id={"tp": lax.rem(rank + k, ranks)}, device_id_type=MESH)
 
     mask = (lax.broadcasted_iota(jnp.int32, (width, width), 0) // head
             == lax.broadcasted_iota(jnp.int32, (width, width), 1) // head)
@@ -135,6 +137,18 @@
         return carry
 
     lax.fori_loop(0, last, step, 0)
+
+    @pl.when(own)
+    def _():
+        local.wait()
+        for k in range(1, n):
+            c = lax.rem(me + k, n)
+            pltpu.make_async_remote_copy(
+                src_ref=pieces_ref.at[0], dst_ref=mine_ref.at[c],
+                send_sem=piece_send.at[0], recv_sem=piece_recv.at[c],
+                device_id={"ctx": c}, device_id_type=MESH).wait_recv()
+        for k in range(1, ranks):
+            mine_copy(k).start()
 
     state = [None] * groups
     for k in range(CHUNKS - 1, -1, -1):
@@ -238,17 +252,9 @@
 
         lax.fori_loop(0, outer, send, 0)
 
-    @pl.when(own)
-    def _():
-        local.wait()
-
-    for c in range(n):
-        @pl.when(jnp.logical_not(jnp.logical_and(own, me == c)))
-        def _():
-            pltpu.make_async_remote_copy(
-                src_ref=pieces_ref.at[0], dst_ref=mine_ref.at[c],
-                send_sem=piece_send.at[0], recv_sem=piece_recv.at[c],
-                device_id={"ctx": c, "tp": source_rank}, device_id_type=MESH).wait_recv()
+    @pl.when(jnp.logical_not(own))
+    def _():
+        mine_copy(1).wait_recv()
 
     total[...] = jnp.zeros_like(total)
 
@@ -292,10 +298,14 @@
         copy.wait_send()
 
     for p in range(pieces):
-        for t in range(ranks):
-            @pl.when(to_other(p, t))
-            def _():
-                piece_copy(p, t).wait_send()
+        @pl.when(rank * pieces + p != me)
+        def _():
+            piece_copy(p).wait_send()
+
+    @pl.when(own)
+    def _():
+        for k in range(1, ranks):
+            mine_copy(k).wait_send()
 
     def drain(o, carry):
         for g in range(groups):
@@ -348,8 +358,10 @@
             pltpu.SemaphoreType.DMA,
             pltpu.SemaphoreType.DMA,
             pltpu.SemaphoreType.DMA,
-            pltpu.SemaphoreType.DMA((pieces * ranks,)),
+            pltpu.SemaphoreType.DMA((pieces,)),
             pltpu.SemaphoreType.DMA((n,)),
+            pltpu.SemaphoreType.DMA((ranks,)),
+            pltpu.SemaphoreType.DMA,
             pltpu.SemaphoreType.DMA((groups, n // 2)),
             pltpu.SemaphoreType.DMA((groups, n // 2)),
             pltpu.SemaphoreType.DMA((n, groups)),

time: 99.6 us -> 84.9 us (0.85)
  Pallas kernels: 95.4 us -> 81 us
    pallas_call x1, Pallas kernels: 95.4 us -> 81 us  [on_device(): pl.pallas_call(backward, out_shape=jax.ShapeDtypeStruct((columns // ranks...]
where the time goes in v4:
time: 84.9 us; the launch traced here: 84 us
  Pallas kernels  81 us (95%)
  local copies, waits for them, and re-layouts  3 us (4%)
    pallas_call x1, Pallas kernels, on_device(): pl.pallas_call(backward, out_shape=jax.ShapeDtypeStruct((columns // ranks...  81 us

profile of v4, /device:TPU:0, one launch (start us, length us, event | category | flops | bytes accessed | tf_op | source)
XLA Modules:
  0.0 84.0 jit_solution(4152580405171370525)
XLA Ops:
  0.0 0.0 copy-start.2
  0.0 1.1 %copy.6 = bf16[512,192]{1,0:T(8,128)(2,1)S(1)} copy(bf16[512,192]{0,1:T(8,128)(2,1)} %bitcast.5) | data formatting | bytes 393216 | tf_op jit(solution)/shard_map/transpose | solution.py:337
  1.1 0.0 copy-done.2
  1.1 0.0 copy-start
  1.1 0.0 copy-start.1
  1.1 0.2 copy.5
  1.3 0.1 reshape.6.weights_ref
  1.4 0.7 copy-done
  2.1 0.1 copy-done.1
  2.2 81.0 %shard_map.46 = f32[64,2048]{1,0:T(8,128)S(1)} custom-call(f32[192,512]{1,0:T(8,128)S(1)} %copy-done, f32[192,512]{1,0:T(8,128)S(1)} %copy-done.1, f32[64,512]{1,0:T(8,128)S(1)} %reshape.6.weights_ref, bf16[2,256,192]{2,1,0:T(8,128)(2,1)S(1)} %bitcast.3), custom_call_target="tpu_custom_call" | custom-call | tf_op jit(solution)/shard_map/pallas_call | solution.py:340
  83.2 0.8 copy.8
Async XLA Ops:
  0.0 1.1 %copy-start.2 = (f32[8,64,64]{2,1,0:T(8,128)S(1)}, f32[8,64,64]{2,1,0:T(8,128)}, u32[]{:S(2)}) copy-start(f32[8,64,64]{2,1,0:T(8,128)} %param.7) | copy-start | bytes 393220
  1.1 1.0 %copy-start = (f32[192,512]{1,0:T(8,128)S(1)}, f32[192,512]{1,0:T(8,128)}, u32[]{:S(2)}) copy-start(f32[192,512]{1,0:T(8,128)} %states_ref.1) | copy-start | bytes 1179652
  1.1 1.1 %copy-start.1 = (f32[192,512]{1,0:T(8,128)S(1)}, f32[192,512]{1,0:T(8,128)}, u32[]{:S(2)}) copy-start(f32[192,512]{1,0:T(8,128)} %cot_ref.1) | copy-start | bytes 1179652

commit v5 on v4

--- a/solution.py
+++ b/solution.py
@@ -261,7 +261,6 @@
     def gather(i, carry):
         o = outer - 1 - i
         near = 2 * o + lax.rem(me, 2)
-        far = 2 * o + 1 - lax.rem(me, 2)
 
         @pl.when(o != place)
         def _():
@@ -269,29 +268,36 @@
                 arrived(near, g)
                 pair_copy(g, o).start()
 
-        for c in (near, far):
-            for g in range(groups):
-                lanes = slice(g * width, (g + 1) * width)
-                if c is far:
-                    arrived(far, g)
-                total[:, lanes] += dot(mine_ref[c], blocks[c, g])
+        for g in range(groups):
+            total[:, g * width:(g + 1) * width] += dot(mine_ref[near], blocks[near, g])
         return carry
 
     lax.fori_loop(0, outer, gather, 0)
 
     share = total.shape[0] // ranks
 
-    def rows_copy(t, source):
-        return pltpu.make_async_remote_copy(
-            src_ref=total.at[pl.ds(t * share, share)],
-            dst_ref=out_ref.at[:, pl.ds(pl.multiple_of(source * units, 128), units)],
-            send_sem=rows_send.at[t], recv_sem=rows_recv.at[source],
+    def rows_copy(t, source, g):
+        start = pl.multiple_of(source * units + g * width, 128)
+        return pltpu.make_async_remote_copy(
+            src_ref=total.at[pl.ds(t * share, share), pl.ds(g * width, width)],
+            dst_ref=out_ref.at[:, pl.ds(start, width)],
+            send_sem=rows_send.at[g, t], recv_sem=rows_recv.at[g, source],
             device_id={"tp": t}, device_id_type=MESH)
 
-    for k in range(1, ranks):
-        rows_copy(lax.rem(rank + k, ranks), rank).start()
-    out_ref[:, pl.ds(pl.multiple_of(rank * units, 128), units)] = total[
-        pl.ds(pl.multiple_of(rank * share, 8), share), :]
+    for g in range(groups):
+        lanes = slice(g * width, (g + 1) * width)
+
+        def collect(i, carry):
+            far = 2 * (outer - 1 - i) + 1 - lax.rem(me, 2)
+            arrived(far, g)
+            total[:, lanes] += dot(mine_ref[far], blocks[far, g])
+            return carry
+
+        lax.fori_loop(0, outer, collect, 0)
+        for k in range(1, ranks):
+            rows_copy(lax.rem(rank + k, ranks), rank, g).start()
+        out_ref[:, pl.ds(pl.multiple_of(rank * units + g * width, 128), width)] = total[
+            pl.ds(pl.multiple_of(rank * share, 8), share), lanes]
 
     @pl.when(me > 0)
     def _():
@@ -319,8 +325,9 @@
     lax.fori_loop(0, outer, drain, 0)
     for k in range(1, ranks):
         t = lax.rem(rank + k, ranks)
-        rows_copy(t, t).wait_recv()
-        rows_copy(t, rank).wait_send()
+        for g in range(groups):
+            rows_copy(t, t, g).wait_recv()
+            rows_copy(t, rank, g).wait_send()
 
 
 def on_device(layer_inputs, states, cotangent, block_weights):
@@ -365,8 +372,8 @@
             pltpu.SemaphoreType.DMA((groups, n // 2)),
             pltpu.SemaphoreType.DMA((groups, n // 2)),
             pltpu.SemaphoreType.DMA((n, groups)),
-            pltpu.SemaphoreType.DMA((ranks,)),
-            pltpu.SemaphoreType.DMA((ranks,)),
+            pltpu.SemaphoreType.DMA((groups, ranks)),
+            pltpu.SemaphoreType.DMA((groups, ranks)),
         ],
         compiler_params=pltpu.CompilerParams(
             collective_id=0, has_side_effects=True, vmem_limit_bytes=48 * 1024 * 1024),

time: 84.9 us -> 79.5 us (0.936)
  Pallas kernels: 81 us -> 75.8 us
    pallas_call x1, Pallas kernels: 81 us -> 75.8 us  [on_device(): pl.pallas_call(backward, out_shape=jax.ShapeDtypeStruct((columns // ranks...]
where the time goes in v5:
time: 79.5 us; the launch traced here: 78.8 us
  Pallas kernels  75.8 us (95%)
  local copies, waits for them, and re-layouts  3 us (4%)
    pallas_call x1, Pallas kernels, on_device(): pl.pallas_call(backward, out_shape=jax.ShapeDtypeStruct((columns // ranks...  75.8 us
    unnamed x7, local copies, waits for them, and re-layouts  1.62 us

profile of v5, /device:TPU:0, one launch (start us, length us, event | category | flops | bytes accessed | tf_op | source)
XLA Modules:
  0.0 78.8 jit_solution(3850812285280174162)
XLA Ops:
  0.0 0.0 copy-start.2
  0.0 1.1 %copy.6 = bf16[512,192]{1,0:T(8,128)(2,1)S(1)} copy(bf16[512,192]{0,1:T(8,128)(2,1)} %bitcast.5) | data formatting | bytes 393216 | tf_op jit(solution)/shard_map/transpose | solution.py:344
  1.1 0.0 copy-done.2
  1.1 0.0 copy-start
  1.1 0.0 copy-start.1
  1.1 0.2 copy.5
  1.3 0.1 reshape.6.weights_ref
  1.4 0.7 copy-done
  2.1 0.1 copy-done.1
  2.2 75.8 %shard_map.46 = f32[64,2048]{1,0:T(8,128)S(1)} custom-call(f32[192,512]{1,0:T(8,128)S(1)} %copy-done, f32[192,512]{1,0:T(8,128)S(1)} %copy-done.1, f32[64,512]{1,0:T(8,128)S(1)} %reshape.6.weights_ref, bf16[2,256,192]{2,1,0:T(8,128)(2,1)S(1)} %bitcast.3), custom_call_target="tpu_custom_call" | custom-call | tf_op jit(solution)/shard_map/pallas_call | solution.py:347
  78.0 0.8 %copy.8 = f32[64,2048]{1,0:T(8,128)} copy(f32[64,2048]{1,0:T(8,128)S(1)} %shard_map.46) | data formatting | bytes 1048576
Async XLA Ops:
  0.0 1.1 %copy-start.2 = (f32[8,64,64]{2,1,0:T(8,128)S(1)}, f32[8,64,64]{2,1,0:T(8,128)}, u32[]{:S(2)}) copy-start(f32[8,64,64]{2,1,0:T(8,128)} %param.7) | copy-start | bytes 393220
  1.1 1.0 %copy-start = (f32[192,512]{1,0:T(8,128)S(1)}, f32[192,512]{1,0:T(8,128)}, u32[]{:S(2)}) copy-start(f32[192,512]{1,0:T(8,128)} %states_ref.1) | copy-start | bytes 1179652
  1.1 1.1 %copy-start.1 = (f32[192,512]{1,0:T(8,128)S(1)}, f32[192,512]{1,0:T(8,128)}, u32[]{:S(2)}) copy-start(f32[192,512]{1,0:T(8,128)} %cot_ref.1) | copy-start | bytes 1179652

commit v6 on v5

--- a/solution.py
+++ b/solution.py
@@ -35,7 +35,7 @@
 def backward(states_ref, cot_ref, weights_ref, pieces_ref, out_ref,
              maps, weights, relay_weights, suffix, suffix_vec, spread_e, full, mine_ref, blocks,
              total, e_in, e_out, send_sem, recv_sem, local_sem, piece_send, piece_recv,
-             mine_send, mine_recv, line_send, pair_send, block_recv, rows_send, rows_recv):
+             mine_send, mine_recv, line_send, far_send, pair_send, block_recv, rows_send, rows_recv):
     n = lax.axis_size("ctx")
     ranks = lax.axis_size("tp")
     me = lax.axis_index("ctx")
@@ -66,11 +66,13 @@
     for k in range(1, outer):
         pl.semaphore_signal(barrier, inc=1, device_id={"ctx": lax.rem(me + 2 * k, n)},
                             device_id_type=MESH)
+        pl.semaphore_signal(barrier, inc=1, device_id={"ctx": lax.rem(across + 2 * k, n)},
+                            device_id_type=MESH)
     for k in range(1, ranks):
         pl.semaphore_signal(barrier, inc=1, device_id={"tp": lax.rem(rank + k, ranks)},
                             device_id_type=MESH)
     pl.semaphore_wait(
-        barrier, 2 + 1 + outer - 1 + ranks - 1 + pieces - own.astype(jnp.int32))
+        barrier, 2 + 1 + 2 * (outer - 1) + ranks - 1 + pieces - own.astype(jnp.int32))
 
     def piece_copy(p):
         return pltpu.make_async_remote_copy(
@@ -214,6 +216,12 @@
             send_sem=line_send.at[g, o], recv_sem=block_recv.at[me, g],
             device_id={"ctx": 2 * o + lax.rem(me, 2)}, device_id_type=MESH)
 
+    def far_copy(g, o):
+        return pltpu.make_async_remote_copy(
+            src_ref=blocks.at[me, g], dst_ref=blocks.at[me, g],
+            send_sem=far_send.at[g, o], recv_sem=block_recv.at[me, g],
+            device_id={"ctx": 2 * o + 1 - lax.rem(me, 2)}, device_id_type=MESH)
+
     def pair_copy(g, o):
         c = 2 * o + lax.rem(me, 2)
         return pltpu.make_async_remote_copy(
@@ -248,6 +256,10 @@
             @pl.when(o != place)
             def _():
                 line_copy(g, o).start()
+
+            @pl.when(o < place)
+            def _():
+                far_copy(g, o).start()
             return carry
 
         lax.fori_loop(0, outer, send, 0)
@@ -266,7 +278,10 @@
         def _():
             for g in range(groups):
                 arrived(near, g)
-                pair_copy(g, o).start()
+
+                @pl.when(o < place)
+                def _():
+                    pair_copy(g, o).start()
 
         for g in range(groups):
             total[:, g * width:(g + 1) * width] += dot(mine_ref[near], blocks[near, g])
@@ -315,7 +330,13 @@
 
     def drain(o, carry):
         for g in range(groups):
-            pair_copy(g, o).wait_send()
+            @pl.when(o <= place)
+            def _():
+                pair_copy(g, o).wait_send()
+
+            @pl.when(o < place)
+            def _():
+                far_copy(g, o).wait_send()
 
             @pl.when(o != place)
             def _():
@@ -371,6 +392,7 @@
             pltpu.SemaphoreType.DMA,
             pltpu.SemaphoreType.DMA((groups, n // 2)),
             pltpu.SemaphoreType.DMA((groups, n // 2)),
+            pltpu.SemaphoreType.DMA((groups, n // 2)),
             pltpu.SemaphoreType.DMA((n, groups)),
             pltpu.SemaphoreType.DMA((groups, ranks)),
             pltpu.SemaphoreType.DMA((groups, ranks)),

time: 79.5 us -> 84 us (1.057)
  the two profiles are of different devices: /device:TPU:0 before, /device:TPU:15 now
where the time goes in v6:
time: 84 us; the launch traced here: 83.9 us
  Pallas kernels  80.9 us (96%)
  local copies, waits for them, and re-layouts  3 us (4%)
    pallas_call x1, Pallas kernels, on_device(): pl.pallas_call(backward, out_shape=jax.ShapeDtypeStruct((columns // ranks...  80.9 us

profile of v6, /device:TPU:15, one launch (start us, length us, event | category | flops | bytes accessed | tf_op | source)
XLA Modules:
  0.0 83.9 jit_solution(5747336282436440184)
XLA Ops:
  0.0 0.0 copy-start.2
  0.0 1.1 %copy.6 = bf16[512,192]{1,0:T(8,128)(2,1)S(1)} copy(bf16[512,192]{0,1:T(8,128)(2,1)} %bitcast.5) | data formatting | bytes 393216 | tf_op jit(solution)/shard_map/transpose | solution.py:365
  1.1 0.0 copy-done.2
  1.1 0.0 copy-start
  1.1 0.0 copy-start.1
  1.1 0.2 copy.5
  1.3 0.1 reshape.6.weights_ref
  1.4 0.7 copy-done
  2.1 0.1 copy-done.1
  2.2 80.9 %shard_map.46 = f32[64,2048]{1,0:T(8,128)S(1)} custom-call(f32[192,512]{1,0:T(8,128)S(1)} %copy-done, f32[192,512]{1,0:T(8,128)S(1)} %copy-done.1, f32[64,512]{1,0:T(8,128)S(1)} %reshape.6.weights_ref, bf16[2,256,192]{2,1,0:T(8,128)(2,1)S(1)} %bitcast.3), custom_call_target="tpu_custom_call" | custom-call | tf_op jit(solution)/shard_map/pallas_call | solution.py:368
  83.1 0.8 copy.8
Async XLA Ops:
  0.0 1.1 %copy-start.2 = (f32[8,64,64]{2,1,0:T(8,128)S(1)}, f32[8,64,64]{2,1,0:T(8,128)}, u32[]{:S(2)}) copy-start(f32[8,64,64]{2,1,0:T(8,128)} %param.7) | copy-start | bytes 393220
  1.1 1.0 %copy-start = (f32[192,512]{1,0:T(8,128)S(1)}, f32[192,512]{1,0:T(8,128)}, u32[]{:S(2)}) copy-start(f32[192,512]{1,0:T(8,128)} %states_ref.1) | copy-start | bytes 1179652
  1.1 1.1 %copy-start.1 = (f32[192,512]{1,0:T(8,128)S(1)}, f32[192,512]{1,0:T(8,128)}, u32[]{:S(2)}) copy-start(f32[192,512]{1,0:T(8,128)} %cot_ref.1) | copy-start | bytes 1179652

commit v7 on v5

--- a/solution.py
+++ b/solution.py
@@ -252,10 +252,6 @@
 
         lax.fori_loop(0, outer, send, 0)
 
-    @pl.when(jnp.logical_not(own))
-    def _():
-        mine_copy(1).wait_recv()
-
     total[...] = jnp.zeros_like(total)
 
     def gather(i, carry):
@@ -268,11 +264,21 @@
                 arrived(near, g)
                 pair_copy(g, o).start()
 
+        return carry
+
+    lax.fori_loop(0, outer, gather, 0)
+
+    @pl.when(jnp.logical_not(own))
+    def _():
+        mine_copy(1).wait_recv()
+
+    def multiply(i, carry):
+        near = 2 * (outer - 1 - i) + lax.rem(me, 2)
         for g in range(groups):
             total[:, g * width:(g + 1) * width] += dot(mine_ref[near], blocks[near, g])
         return carry
 
-    lax.fori_loop(0, outer, gather, 0)
+    lax.fori_loop(0, outer, multiply, 0)
 
     share = total.shape[0] // ranks
 

time: 79.5 us -> 76.7 us (0.965)
  Pallas kernels: 75.8 us -> 72.5 us
    pallas_call x1, Pallas kernels: 75.8 us -> 72.5 us  [on_device(): pl.pallas_call(backward, out_shape=jax.ShapeDtypeStruct((columns // ranks...]
where the time goes in v7:
time: 76.7 us; the launch traced here: 75.5 us
  Pallas kernels  72.5 us (95%)
  local copies, waits for them, and re-layouts  3 us (4%)
    pallas_call x1, Pallas kernels, on_device(): pl.pallas_call(backward, out_shape=jax.ShapeDtypeStruct((columns // ranks...  72.5 us
    unnamed x7, local copies, waits for them, and re-layouts  1.62 us

profile of v7, /device:TPU:0, one launch (start us, length us, event | category | flops | bytes accessed | tf_op | source)
XLA Modules:
  0.0 75.5 jit_solution(11092094979668520772)
XLA Ops:
  0.0 0.0 copy-start.2
  0.0 1.1 %copy.6 = bf16[512,192]{1,0:T(8,128)(2,1)S(1)} copy(bf16[512,192]{0,1:T(8,128)(2,1)} %bitcast.5) | data formatting | bytes 393216 | tf_op jit(solution)/shard_map/transpose | solution.py:350
  1.1 0.0 copy-done.2
  1.1 0.0 copy-start
  1.1 0.0 copy-start.1
  1.1 0.2 copy.5
  1.3 0.1 reshape.6.weights_ref
  1.4 0.7 copy-done
  2.1 0.1 copy-done.1
  2.2 72.5 %shard_map.46 = f32[64,2048]{1,0:T(8,128)S(1)} custom-call(f32[192,512]{1,0:T(8,128)S(1)} %copy-done, f32[192,512]{1,0:T(8,128)S(1)} %copy-done.1, f32[64,512]{1,0:T(8,128)S(1)} %reshape.6.weights_ref, bf16[2,256,192]{2,1,0:T(8,128)(2,1)S(1)} %bitcast.3), custom_call_target="tpu_custom_call" | custom-call | tf_op jit(solution)/shard_map/pallas_call | solution.py:353
  74.7 0.8 %copy.8 = f32[64,2048]{1,0:T(8,128)} copy(f32[64,2048]{1,0:T(8,128)S(1)} %shard_map.46) | data formatting | bytes 1048576
Async XLA Ops:
  0.0 1.1 %copy-start.2 = (f32[8,64,64]{2,1,0:T(8,128)S(1)}, f32[8,64,64]{2,1,0:T(8,128)}, u32[]{:S(2)}) copy-start(f32[8,64,64]{2,1,0:T(8,128)} %param.7) | copy-start | bytes 393220
  1.1 1.0 %copy-start = (f32[192,512]{1,0:T(8,128)S(1)}, f32[192,512]{1,0:T(8,128)}, u32[]{:S(2)}) copy-start(f32[192,512]{1,0:T(8,128)} %states_ref.1) | copy-start | bytes 1179652
  1.1 1.1 %copy-start.1 = (f32[192,512]{1,0:T(8,128)S(1)}, f32[192,512]{1,0:T(8,128)}, u32[]{:S(2)}) copy-start(f32[192,512]{1,0:T(8,128)} %cot_ref.1) | copy-start | bytes 1179652
